TPU v7x, 32 devices: a whole 2x2x4 slice. The times are simulated.
32 devices in a mesh: dp: 4 (over z), mp: 8 (over y, x, core).
Axes of the slice: x: 2, y: 2, z: 4, core: 2. Of those that a mesh axis runs over, the one named last changes fastest.
Arguments:
- gradients: bfloat16 [4, 2, 768, 2048], P('dp', None, None, 'mp'), may hold values from -4 to 4
- weights: bfloat16 [2, 768, 2048], P(None, None, 'mp'), may hold values from -4 to 4
- projection: float32 [2, 768, 256], replicated, may hold values from -0.21875 to 0.21875
- moment_first: float32 [2, 256, 2048], P(None, 'dp', 'mp'), may hold values from -6 to 6
- moment_second: float32 [2, 256, 2048], P(None, 'dp', 'mp'), may hold values from 0.25 to 4
Outputs:
- new_weights: bfloat16 [2, 768, 2048], P(None, None, 'mp')
- new_first: float32 [2, 256, 2048], P(None, 'dp', 'mp')
- new_second: float32 [2, 256, 2048], P(None, 'dp', 'mp')
- new_bases: float32 [2, 768, 256], replicated
All inputs are finite; a program needn't handle non-finite values.
Results may differ from a plain program's by a relative error of at most 0.0004.
Values may be sent and summed in bfloat16 or wider, within the bound.
A program may use at most 64 MiB of HBM per device.

v0:
```python
import jax
import jax.numpy as jnp
from jax import lax
from jax.sharding import PartitionSpec as P

NS_ITERS = 4
beta_first = 0.5
beta_second = 0.5
adam_eps = 1e-06
learn_rate = 0.1


def newton_schulz(subspace):
    highest = lax.Precision.HIGHEST
    factor = 1.0 / (jnp.sqrt(jnp.sum(subspace * subspace, axis=(1, 2), keepdims=True)) + 1e-06)
    current = subspace * factor
    for sweep in range(NS_ITERS):
        gram = jnp.einsum("ldr,lds->lrs", current, current, precision=highest)
        current = 1.5 * current - 0.5 * jnp.einsum("ldr,lrs->lds", current, gram, precision=highest)
    return current


def back_project(bases_rows, direction_own):
    highest = lax.Precision.HIGHEST
    return jnp.einsum(
        "ldr,lrf->ldf",
        bases_rows,
        lax.all_gather(direction_own, "dp", axis=1, tiled=True),
        precision=highest,
    )


def shards(gradients, weights, projection, moment_first, moment_second):
    highest = lax.Precision.HIGHEST
    local_grad = gradients[0].astype(jnp.float32)
    totals = lax.psum(local_grad, "dp")
    lowrank = jnp.einsum("ldr,ldf->lrf", projection, totals, precision=highest)
    partial_sub = jnp.einsum("ldf,lrf->ldr", totals, lowrank, precision=highest)
    subspace = lax.psum(partial_sub, "mp")
    rank_rows = moment_first.shape[1]
    rank_start = lax.axis_index("dp") * rank_rows
    low_own = lax.dynamic_slice_in_dim(lowrank, rank_start, rank_rows, 1)
    new_first = beta_first * moment_first + (1.0 - beta_first) * low_own
    new_second = beta_second * moment_second + (1.0 - beta_second) * low_own * low_own
    direction_own = new_first / (jnp.sqrt(new_second) + adam_eps)
    width_rows = weights.shape[1] // lax.axis_size("dp")
    row_start = lax.axis_index("dp") * width_rows
    bases_rows = lax.dynamic_slice_in_dim(projection, row_start, width_rows, 1)
    weight_rows = lax.dynamic_slice_in_dim(weights, row_start, width_rows, 1)
    delta_rows = back_project(bases_rows, direction_own)
    updated = (weight_rows.astype(jnp.float32) - learn_rate * delta_rows).astype(jnp.bfloat16)
    new_weights = lax.all_gather(updated, "dp", axis=1, tiled=True)
    new_bases = newton_schulz(subspace)
    return (new_weights, new_first, new_second, new_bases)


def solution(mesh):
    placed = (
        P("dp", None, None, "mp"),
        P(None, None, "mp"),
        P(),
        P(None, "dp", "mp"),
        P(None, "dp", "mp"),
    )
    return jax.shard_map(
        shards,
        mesh=mesh,
        in_specs=placed,
        out_specs=(P(None, None, "mp"), P(None, "dp", "mp"), P(None, "dp", "mp"), P()),
        check_vma=False,
    )
```

profile of v0, /device:TPU:0, one launch (start us, length us, event | category | flops | bytes accessed | tf_op | source)
XLA Modules:
  0.0 174.0 jit_solution(6145538785186923639)
XLA Ops:
  7.2 2.5 %bitcast_convert_fusion = f32[2,768,256]{2,1,0:T(8,128)} fusion(bf16[1,2,768,256]{3,2,1,0:T(8,128)(2,1)} %param.5), kind=kLoop, calls=%fused_computation.12 | loop fusion | flops 393216 | bytes 2359296 | tf_op jit(solution)/shard_map/convert_element_type | solution.py:35
  9.8 0.0 all-reduce.5.cloned.1.call-start
  9.8 72.8 %all-reduce.3.cloned.1.call-done = f32[2,768,256]{2,1,0:T(8,128)} async-done(((f32[2,768,256]{2,1,0:T(8,128)}), f32[2,768,256]{2,1,0:T(8,128)}) %all-reduce.3.cloned.1.call-update) | async-done | bytes 1572880 | tf_op jit(solution)/shard_map/psum | solution.py:36
  82.7 4.2 %fusion.11 = f32[2,256,256]{2,1,0:T(8,128)S(1)} fusion(f32[2,768,256]{2,1,0:T(8,128)S(1)} %copy-done, f32[2,768,256]{2,1,0:T(8,128)} %all-reduce.3.cloned.1.call-done), kind=kOutput, calls=%fused_computation.22 | convolution fusion | flops 1207959552 | bytes 3670016 | tf_op jit(solution)/shard_map/ldr,ldf->lrf/dot_general | solution.py:37
  86.9 2.6 %convolution_bitcast_fusion = f32[2,768,256]{1,2,0:T(8,128)} fusion(f32[2,256,256]{2,1,0:T(8,128)S(1)} %fusion.11, f32[2,768,256]{2,1,0:T(8,128)S(1)} %copy-done.2), kind=kOutput, calls=%fused_computation.5 | convolution fusion | flops 1207959552 | bytes 3670016 | tf_op jit(solution)/shard_map/ldf,lrf->ldr/dot_general | solution.py:38
  89.5 0.9 copy-done.3
  90.4 0.1 copy-done.4
  90.5 0.8 add_divide_fusion
  91.2 15.7 %all_gather.6 = f32[2,256,256]{2,1,0:T(8,128)S(1)} all-gather(f32[2,64,256]{2,1,0:T(8,128)S(1)} %get-tuple-element.8), channel_id=1, replica_groups=mesh['dp'=4,'mp'=8] {'dp'}, dimensions={1}, use_global_device_ids=true | all-gather | bytes 655360 | tf_op jit(solution)/shard_map/all_gather | solution.py:28
  106.9 1.5 fusion.4
  108.4 18.3 %all_gather.7 = bf16[2,768,256]{2,1,0:T(8,128)(2,1)} all-gather(bf16[2,192,256]{2,1,0:T(8,128)(2,1)S(1)} %fusion.4), channel_id=1, replica_groups=mesh['dp'=4,'mp'=8] {'dp'}, dimensions={1}, use_global_device_ids=true | all-gather | bytes 983040 | tf_op jit(solution)/shard_map/all_gather | solution.py:52
  126.7 20.9 %all-reduce.5.cloned.1.call-done = f32[2,768,256]{1,2,0:T(8,128)} async-done(((f32[2,768,256]{1,2,0:T(8,128)}), f32[2,768,256]{1,2,0:T(8,128)}) %all-reduce.5.cloned.1.call-update) | async-done | bytes 1572880 | tf_op jit(solution)/shard_map/psum | solution.py:39
  147.6 1.8 %multiply_reduce_fusion = f32[2]{0:T(128)S(1)} fusion(f32[2,768,256]{1,2,0:T(8,128)} %all-reduce.5.cloned.1.call-done), kind=kLoop, calls=%fused_computation.4 | loop fusion | flops 786430 | bytes 1572872 | tf_op jit(solution)/shard_map/reduce_sum | solution.py:15
  149.4 0.0 copy-done.1
  149.5 1.8 %fusion = f32[2,256,256]{2,1,0:T(8,128)S(1)} fusion(f32[2,768,256]{1,2,0:T(8,128)S(1)} %copy-done.1, f32[2]{0:T(128)S(1)} %add_divide_fusion.1), kind=kOutput, calls=%fused_computation.6 | convolution fusion | flops 1208352768 | bytes 2097160 | tf_op jit(solution)/shard_map/ldr,lds->lrs/dot_general | solution.py:18
  151.2 2.0 %multiply_subtract_fusion.3 = f32[2,768,256]{1,2,0:T(8,128)S(1)} fusion(f32[2,256,256]{2,1,0:T(8,128)S(1)} %fusion, f32[2,768,256]{1,2,0:T(8,128)S(1)} %copy-done.1, f32[2]{0:T(128)S(1)} %add_divide_fusion.1), kind=kOutput, calls=%fused_computation.3 | convolution fusion | flops 1209925632 | bytes 3670024 | tf_op jit(solution)/shard_map/ldr,lrs->lds/dot_general | solution.py:19
  153.2 1.6 fusion.12
  154.9 1.8 %multiply_subtract_fusion.2 = f32[2,768,256]{1,2,0:T(8,128)S(1)} fusion(f32[2,768,256]{1,2,0:T(8,128)S(1)} %multiply_subtract_fusion.3, f32[2,256,256]{2,1,0:T(8,128)S(1)} %fusion.12), kind=kOutput, calls=%fused_computation.2 | convolution fusion | flops 1209139200 | bytes 3670016 | tf_op jit(solution)/shard_map/ldr,lrs->lds/dot_general | solution.py:19
  156.6 1.6 fusion.13
  158.3 1.8 %multiply_subtract_fusion.1 = f32[2,768,256]{1,2,0:T(8,128)S(1)} fusion(f32[2,768,256]{1,2,0:T(8,128)S(1)} %multiply_subtract_fusion.2, f32[2,256,256]{2,1,0:T(8,128)S(1)} %fusion.13), kind=kOutput, calls=%fused_computation.1 | convolution fusion | flops 1209139200 | bytes 3670016 | tf_op jit(solution)/shard_map/ldr,lrs->lds/dot_general | solution.py:19
  160.1 1.6 fusion.14
  161.7 1.8 %multiply_subtract_fusion = f32[2,768,256]{1,2,0:T(8,128)S(1)} fusion(f32[2,768,256]{1,2,0:T(8,128)S(1)} %multiply_subtract_fusion.1, f32[2,256,256]{2,1,0:T(8,128)S(1)} %fusion.14), kind=kOutput, calls=%fused_computation | convolution fusion | flops 1209139200 | bytes 3670016 | tf_op jit(solution)/shard_map/ldr,lrs->lds/dot_general | solution.py:19
  163.5 1.6 copy.18
  165.1 2.1 %copy.31 = bf16[2,768,256]{2,1,0:T(8,128)(2,1)} copy(bf16[2,768,256]{2,1,0:T(8,128)(2,1)} %all_gather.7) | data formatting | bytes 1572864
  (11 shorter events, 0.1 us)
Async XLA Ops:
  7.2 75.5 %copy-start = (f32[2,768,256]{2,1,0:T(8,128)S(1)}, f32[2,768,256]{2,1,0:T(8,128)}, u32[]{:S(2)}) copy-start(f32[2,768,256]{2,1,0:T(8,128)} %param.7) | copy-start | bytes 4718596
  7.2 75.5 %all-reduce.3.cloned.1.call-start = ((), (), s32[]{:S(2)}) async-start(), calls=%async_computation | async-start | bytes 3145728 | tf_op jit(solution)/shard_map/psum | solution.py:36
  9.8 137.8 %all-reduce.5.cloned.1.call-start = ((), (), s32[]{:S(2)}) async-start(), calls=%async_computation.1 | async-start | bytes 3145728 | tf_op jit(solution)/shard_map/psum | solution.py:39
  82.7 4.2 %copy-start.2 = (f32[2,768,256]{2,1,0:T(8,128)S(1)}, f32[2,768,256]{2,1,0:T(8,128)}, u32[]{:S(2)}) copy-start(f32[2,768,256]{2,1,0:T(8,128)} %all-reduce.3.cloned.1.call-done) | copy-start | bytes 4718596
  89.5 0.9 copy-start.3
  89.5 1.0 copy-start.4
  147.6 1.9 %copy-start.1 = (f32[2,768,256]{1,2,0:T(8,128)S(1)}, f32[2,768,256]{1,2,0:T(8,128)}, u32[]{:S(2)}) copy-start(f32[2,768,256]{1,2,0:T(8,128)} %all-reduce.5.cloned.1.call-done) | copy-start | bytes 4718596
Sparse Core Ops, SparseCore 0:
  10.9 71.6 all-reduce.2
  89.7 57.8 all-reduce.4
where the time goes:
time: 174 us
  waiting for transfers between devices  93.7 us (54%)
  blocking collectives  34 us (20%)
  matrix products  22.3 us (13%)
  between operations  14.1 us (8%)
  other arithmetic  5.1 us (3%)
  local copies, waits for them, and re-layouts  4.67 us (3%)
    psum x1, waiting for transfers between devices, shards(): totals = lax.psum(local_grad, 'dp')  72.8 us
    psum x1, waiting for transfers between devices, shards(): subspace = lax.psum(partial_sub, 'mp')  20.9 us
    all_gather x1, blocking collectives, shards(): new_weights = lax.all_gather(updated, 'dp', axis=1, tiled=True)  18.3 us
    all_gather x1, blocking collectives, back_project(): lax.all_gather(direction_own, 'dp', axis=1, tiled=True)  15.7 us
    dot_general x4, matrix products, newton_schulz(): jnp.einsum('ldr,lrs->lds', current, gram, precision=highest)  7.29 us
    dot_general x4, matrix products, newton_schulz(): gram = jnp.einsum('ldr,lds->lrs', current, current, precision=highest)  6.66 us
    unnamed x12, local copies, waits for them, and re-layouts  4.67 us
    dot_general x1, matrix products, shards(): lowrank = jnp.einsum('ldr,ldf->lrf', projection, totals, precision=highest)  4.21 us
  transfers between devices with their start and end apart: 2, of which 2 were waited for; matrix products, arithmetic and copies ran while one was open for 1% of the time, Pallas kernels for 0%

commit v1 on v0

--- a/solution.py
+++ b/solution.py
@@ -33,7 +33,10 @@
 def shards(gradients, weights, projection, moment_first, moment_second):
     highest = lax.Precision.HIGHEST
     local_grad = gradients[0].astype(jnp.float32)
-    totals = lax.psum(local_grad, "dp")
+    devices, totals = (lax.axis_size("dp"), local_grad)
+    for far in [1 << k for k in range(devices.bit_length() - 1)]:
+        swap = [(i, i ^ far) for i in range(devices)]
+        totals = totals + lax.ppermute(totals, "dp", swap)
     lowrank = jnp.einsum("ldr,ldf->lrf", projection, totals, precision=highest)
     partial_sub = jnp.einsum("ldf,lrf->ldr", totals, lowrank, precision=highest)
     subspace = lax.psum(partial_sub, "mp")

time: 174 us -> 213 us (1.22)
  waiting for transfers between devices: 93.7 us -> 124 us
  starting transfers between devices: 0.08 us -> 5.97 us
  matrix products: 22.3 us -> 26.3 us
  local copies, waits for them, and re-layouts: 4.67 us -> 1.88 us
    ppermute x0 -> x2, waiting for transfers between devices: none -> 102 us  [shards(): totals = totals + lax.ppermute(totals, 'dp', swap)]
    psum x1 -> x0, waiting for transfers between devices: 72.8 us -> none  [shards(): totals = lax.psum(local_grad, 'dp')]
    ppermute x0 -> x2, starting transfers between devices: none -> 5.94 us  [shards(): totals = totals + lax.ppermute(totals, 'dp', swap)]
    dot_general x4, matrix products: 6.66 us -> 11.3 us  [newton_schulz(): gram = jnp.einsum('ldr,lds->lrs', current, current, precision=highest)]
    unnamed x12 -> x11, local copies, waits for them, and re-layouts: 4.67 us -> 1.88 us
  transfers between devices with their start and end apart: 2 -> 3, of which waited for: 2 -> 3; matrix products, arithmetic and copies ran while one was open for 1% -> 1% of each run, Pallas kernels for 0% -> 0%
where the time goes in v1:
time: 213 us
  waiting for transfers between devices  124 us (58%)
  blocking collectives  34.4 us (16%)
  matrix products  26.3 us (12%)
  between operations  14.1 us (7%)
  starting transfers between devices  5.97 us (3%)
  other arithmetic  5.76 us (3%)
    ppermute x2, waiting for transfers between devices, shards(): totals = totals + lax.ppermute(totals, 'dp', swap)  102 us
    psum x1, waiting for transfers between devices, shards(): subspace = lax.psum(partial_sub, 'mp')  22.2 us
    all_gather x1, blocking collectives, shards(): new_weights = lax.all_gather(updated, 'dp', axis=1, tiled=True)  18.7 us
    all_gather x1, blocking collectives, back_project(): lax.all_gather(direction_own, 'dp', axis=1, tiled=True)  15.7 us
    dot_general x4, matrix products, newton_schulz(): gram = jnp.einsum('ldr,lds->lrs', current, current, precision=highest)  11.3 us
    dot_general x4, matrix products, newton_schulz(): jnp.einsum('ldr,lrs->lds', current, gram, precision=highest)  8.14 us
    ppermute x2, starting transfers between devices, shards(): totals = totals + lax.ppermute(totals, 'dp', swap)  5.94 us
  transfers between devices with their start and end apart: 3, of which 3 were waited for; matrix products, arithmetic and copies ran while one was open for 1% of the time, Pallas kernels for 0%

profile of v1, /device:TPU:0, one launch (start us, length us, event | category | flops | bytes accessed | tf_op | source)
XLA Modules:
  0.0 212.6 jit_solution(7418779889391960890)
XLA Ops:
  7.2 1.4 bitcast_convert_fusion
  8.6 3.1 %collective-permute-start = (f32[2,768,256]{2,1,0:T(8,128)S(1)}, f32[2,768,256]{2,1,0:T(8,128)S(1)}, u32[]{:S(2)}, u32[]{:S(2)}) collective-permute-start(f32[2,768,256]{2,1,0:T(8,128)S(1)} %bitcast_convert_fusion), channel_id=1, source_target_pairs={{0,8},{8,0},{16,24},{24,16},{1,9},{9,1},{17,25},{25,17},{2,10},{10... | collective-permute-start | bytes 4718600 | tf_op jit(solution)/shard_map/ppermute | solution.py:39
  11.8 34.4 %collective-permute-done = f32[2,768,256]{2,1,0:T(8,128)S(1)} collective-permute-done((f32[2,768,256]{2,1,0:T(8,128)S(1)}, f32[2,768,256]{2,1,0:T(8,128)S(1)}, u32[]{:S(2)}, u32[]{:S(2)}) %collective-permute-start) | collective-permute-done | bytes 1572896 | tf_op jit(solution)/shard_map/ppermute | solution.py:39
  46.3 2.8 %collective-permute-start.1 = (f32[2,768,256]{2,1,0:T(8,128)S(1)}, f32[2,768,256]{2,1,0:T(8,128)}, u32[]{:S(2)}, u32[]{:S(2)}) collective-permute-start(f32[2,768,256]{2,1,0:T(8,128)S(1)} %fusion.7), channel_id=1, source_target_pairs={{0,16},{8,24},{16,0},{24,8},{1,17},{9,25},{17,1},{25,9},{2,18},{10... | collective-permute-start | bytes 4718600 | tf_op jit(solution)/shard_map/ppermute | solution.py:39
  49.1 67.5 %collective-permute-done.1 = f32[2,768,256]{2,1,0:T(8,128)} collective-permute-done((f32[2,768,256]{2,1,0:T(8,128)S(1)}, f32[2,768,256]{2,1,0:T(8,128)}, u32[]{:S(2)}, u32[]{:S(2)}) %collective-permute-start.1) | collective-permute-done | bytes 1572896 | tf_op jit(solution)/shard_map/ppermute | solution.py:39
  116.7 1.6 add.37
  118.3 2.7 %fusion.12 = f32[2,256,256]{1,2,0:T(8,128)S(1)} fusion(f32[2,768,256]{2,1,0:T(8,128)S(1)} %add.37, f32[2,768,256]{2,1,0:T(8,128)S(1)} %copy-done), kind=kOutput, calls=%fused_computation.22 | convolution fusion | flops 1207959552 | bytes 3670016 | tf_op jit(solution)/shard_map/ldr,ldf->lrf/dot_general | solution.py:40
  121.0 2.7 %fusion.13 = f32[2,768,256]{2,1,0:T(8,128)} fusion(f32[2,768,256]{2,1,0:T(8,128)S(1)} %add.37, f32[2,256,256]{1,2,0:T(8,128)S(1)} %fusion.12), kind=kOutput, calls=%fused_computation.23 | convolution fusion | flops 1207959552 | bytes 3670016 | tf_op jit(solution)/shard_map/ldf,lrf->ldr/dot_general | solution.py:41
  123.7 0.9 copy-done.3
  124.6 0.8 add_divide_fusion
  125.4 15.7 %all_gather.6 = f32[2,256,256]{2,1,0:T(8,128)S(1)} all-gather(f32[2,64,256]{2,1,0:T(8,128)S(1)} %get-tuple-element.4), channel_id=1, replica_groups=mesh['dp'=4,'mp'=8] {'dp'}, dimensions={1}, use_global_device_ids=true | all-gather | bytes 655360 | tf_op jit(solution)/shard_map/all_gather | solution.py:28
  141.1 1.5 fusion.4
  142.6 18.7 %all_gather.7 = bf16[2,768,256]{2,1,0:T(8,128)(2,1)S(1)} all-gather(bf16[2,192,256]{2,1,0:T(8,128)(2,1)S(1)} %fusion.4), channel_id=1, replica_groups=mesh['dp'=4,'mp'=8] {'dp'}, dimensions={1}, use_global_device_ids=true | all-gather | bytes 983040 | tf_op jit(solution)/shard_map/all_gather | solution.py:55
  161.3 22.2 %all-reduce.2.cloned.1.call-done = f32[2,768,256]{2,1,0:T(8,128)} async-done(((f32[2,768,256]{2,1,0:T(8,128)}), f32[2,768,256]{2,1,0:T(8,128)}) %all-reduce.2.cloned.1.call-update) | async-done | bytes 1572880 | tf_op jit(solution)/shard_map/psum | solution.py:42
  183.6 1.8 multiply_reduce_fusion
  185.4 2.8 %fusion = f32[2,256,256]{2,1,0:T(8,128)S(1)} fusion(f32[2,768,256]{2,1,0:T(8,128)S(1)} %copy-done.1, f32[2]{0:T(128)S(1)} %add_divide_fusion.1), kind=kOutput, calls=%fused_computation.5 | convolution fusion | flops 1208352768 | bytes 2097160 | tf_op jit(solution)/shard_map/ldr,lds->lrs/dot_general | solution.py:18
  188.3 1.7 multiply_subtract_fusion.3
  190.0 2.8 %fusion.14 = f32[2,256,256]{2,1,0:T(8,128)S(1)} fusion(f32[2,768,256]{2,1,0:T(8,128)S(1)} %multiply_subtract_fusion.3), kind=kOutput, calls=%fused_computation.24 | convolution fusion | flops 1207959552 | bytes 2097152 | tf_op jit(solution)/shard_map/ldr,lds->lrs/dot_general | solution.py:18
  192.9 1.7 multiply_subtract_fusion.2
  194.6 2.8 %fusion.15 = f32[2,256,256]{2,1,0:T(8,128)S(1)} fusion(f32[2,768,256]{2,1,0:T(8,128)S(1)} %multiply_subtract_fusion.2), kind=kOutput, calls=%fused_computation.25 | convolution fusion | flops 1207959552 | bytes 2097152 | tf_op jit(solution)/shard_map/ldr,lds->lrs/dot_general | solution.py:18
  197.4 1.9 multiply_subtract_fusion.1
  199.3 2.8 %fusion.16 = f32[2,256,256]{2,1,0:T(8,128)S(1)} fusion(f32[2,768,256]{2,1,0:T(8,128)S(1)} %multiply_subtract_fusion.1), kind=kOutput, calls=%fused_computation.26 | convolution fusion | flops 1207959552 | bytes 2097152 | tf_op jit(solution)/shard_map/ldr,lds->lrs/dot_general | solution.py:18
  202.1 2.8 %multiply_subtract_fusion = f32[2,768,256]{2,1,0:T(8,128)} fusion(f32[2,768,256]{2,1,0:T(8,128)S(1)} %multiply_subtract_fusion.1, f32[2,256,256]{2,1,0:T(8,128)S(1)} %fusion.16), kind=kOutput, calls=%fused_computation | convolution fusion | flops 1209139200 | bytes 3670016 | tf_op jit(solution)/shard_map/ldr,lrs->lds/dot_general | solution.py:19
  204.9 0.9 copy.15
  (13 shorter events, 0.3 us)
Async XLA Ops:
  7.2 111.1 %copy-start = (f32[2,768,256]{2,1,0:T(8,128)S(1)}, f32[2,768,256]{2,1,0:T(8,128)}, u32[]{:S(2)}) copy-start(f32[2,768,256]{2,1,0:T(8,128)} %param.7) | copy-start | bytes 4718596
  7.2 176.4 %all-reduce.2.cloned.1.call-start = ((), (), s32[]{:S(2)}) async-start(), calls=%async_computation | async-start | bytes 3145728 | tf_op jit(solution)/shard_map/psum | solution.py:42
  7.2 38.9 %copy-start.2 = (bf16[1,2,768,256]{3,2,1,0:T(8,128)(2,1)S(1)}, bf16[1,2,768,256]{3,2,1,0:T(8,128)(2,1)}, u32[]{:S(2)}) copy-start(bf16[1,2,768,256]{3,2,1,0:T(8,128)(2,1)} %param.5) | copy-start | bytes 2359300
  8.6 37.5 %collective-permute-start = (f32[2,768,256]{2,1,0:T(8,128)S(1)}, f32[2,768,256]{2,1,0:T(8,128)S(1)}, u32[]{:S(2)}, u32[]{:S(2)}) collective-permute-start(f32[2,768,256]{2,1,0:T(8,128)S(1)} %bitcast_convert_fusion), channel_id=1, source_target_pairs={{0,8},{8,0},{16,24},{24,16},{1,9},{9,1},{17,25},{25,17},{2,10},{10... | collective-permute-start | bytes 4718600 | tf_op jit(solution)/shard_map/ppermute | solution.py:39
  46.3 70.3 %collective-permute-start.1 = (f32[2,768,256]{2,1,0:T(8,128)S(1)}, f32[2,768,256]{2,1,0:T(8,128)}, u32[]{:S(2)}, u32[]{:S(2)}) collective-permute-start(f32[2,768,256]{2,1,0:T(8,128)S(1)} %fusion.7), channel_id=1, source_target_pairs={{0,16},{8,24},{16,0},{24,8},{1,17},{9,25},{17,1},{25,9},{2,18},{10... | collective-permute-start | bytes 4718600 | tf_op jit(solution)/shard_map/ppermute | solution.py:39
  123.6 0.9 copy-start.3
  123.7 1.0 copy-start.4
  183.6 1.9 copy-start.1
Sparse Core Ops, SparseCore 0:
  123.8 59.7 all-reduce.1
